TPU v7x, 256 devices: a whole 4x4x8 slice. The times are simulated.
256 devices in a mesh: dp: 8 (over x, y_hi), seq: 32 (over y_lo, z, core).
Axes of the slice: x: 4, y: 4 (y_hi: 2, y_lo: 2; y = y_hi * 2 + y_lo), z: 8, core: 2. Of those that a mesh axis runs over, the one named last changes fastest.
Arguments:
- inputs: bfloat16 [8, 16384, 1024], P('dp', 'seq'), may hold values from -6 to 6
- out_grad: bfloat16 [8, 16384, 1024], P('dp', 'seq'), may hold values from -6 to 6
- w_in: bfloat16 [1024, 3072], replicated, may hold values from -0.1875 to 0.1875
- taps: float32 [3, 3072], replicated, may hold values from -3 to 3
- filt: bfloat16 [64, 256, 1024], P(None, 'seq'), may hold values from -4 to 4
Outputs:
- mixed: bfloat16 [8, 16384, 1024], P('dp', 'seq')
- in_grad: bfloat16 [8, 16384, 1024], P('dp', 'seq')
- w_in_grad: float32 [1024, 3072], P('dp', 'seq')
- taps_grad: float32 [3, 3072], replicated
All inputs are finite; a program needn't handle non-finite values.
Results may differ from a plain program's by a relative error of at most 0.012.
Values may be sent and summed in bfloat16 or wider, within the bound.
A program may use at most 128 MiB of HBM per device.

v0:
```python
import math
import jax
import jax.numpy as jnp
from jax import lax
from jax.sharding import PartitionSpec as P

BLK = 256


def padded(cells, sides, width):
    for axis, dim in sides:
        count = lax.axis_size(axis)
        ends = count - 1
        head = lax.slice_in_dim(cells, 0, width, axis=dim)
        tail = lax.slice_in_dim(cells, cells.shape[dim] - width, cells.shape[dim], axis=dim)
        cells = jnp.concatenate(
            [
                lax.ppermute(tail, axis, [(i, (i + 1) % count) for i in range(ends)]),
                cells,
                lax.ppermute(head, axis, [((i + 1) % count, i) for i in range(ends)]),
            ],
            axis=dim,
        )
    return cells


def dct_table(count):
    rows = jnp.arange(count, dtype=jnp.float32)[:, None]
    cols = jnp.arange(count, dtype=jnp.float32)[None, :]
    first = jnp.where(rows == 0, jnp.float32(math.sqrt(0.5)), jnp.float32(1.0))
    table = (
        jnp.float32(math.sqrt(2.0 / count))
        * first
        * jnp.cos(jnp.float32(math.pi) * (cols + 0.5) * rows / count)
    )
    return table.astype(jnp.bfloat16)


def block_section(blocks, table_q):
    return jnp.einsum("rq,nbqd->nbrd", table_q, blocks, preferred_element_type=jnp.float32).astype(
        jnp.bfloat16
    )


def span_section(columns, filt, table_p):
    stack, span, narrow, width = columns.shape
    flat = columns.reshape(stack, span, narrow * width)
    second = jnp.einsum("ap,npk->nak", table_p, flat, preferred_element_type=jnp.float32)
    scaled = (filt.reshape(1, span, narrow * width).astype(jnp.float32) * second).astype(
        jnp.bfloat16
    )
    third = jnp.einsum("ap,nak->npk", table_p, scaled, preferred_element_type=jnp.float32).astype(
        jnp.bfloat16
    )
    return third.reshape(columns.shape)


def final_section(blocks, table_q):
    return jnp.einsum("rq,nbrd->nbqd", table_q, blocks, preferred_element_type=jnp.float32)


def shards(inputs, out_grad, w_in, taps, filt):
    tok = inputs.shape[1]
    width = inputs.shape[2]
    nseq = lax.axis_size("seq")
    ndata = lax.axis_size("dp")
    nblocks = tok // BLK
    table_q = dct_table(BLK)
    table_p = dct_table(filt.shape[0])
    factor = 1.0 / math.sqrt(ndata * nseq * tok)
    rows = inputs[0]
    z = jnp.dot(rows, w_in, preferred_element_type=jnp.float32).astype(jnp.bfloat16)
    zpad = padded(z, (("seq", 0),), 1)
    s = taps[0] * zpad[:-2] + taps[1] * zpad[1:-1] + taps[2] * zpad[2:]
    a_part = s[:, :width]
    g_part = s[:, width : 2 * width]
    v_part = s[:, 2 * width :]
    w = (a_part * v_part).astype(jnp.bfloat16)
    gradf = out_grad[0].astype(jnp.float32)
    e4 = (gradf * g_part).astype(jnp.bfloat16)
    columns = lax.all_to_all(
        block_section(w.reshape(1, nblocks, BLK, width), table_q),
        "seq",
        split_axis=2,
        concat_axis=1,
        tiled=True,
    )
    back = lax.all_to_all(
        span_section(columns, filt, table_p), "seq", split_axis=1, concat_axis=2, tiled=True
    )
    h4 = final_section(back, table_q).reshape(tok, width)
    grad_cols = lax.all_to_all(
        block_section(e4.reshape(1, nblocks, BLK, width), table_q),
        "seq",
        split_axis=2,
        concat_axis=1,
        tiled=True,
    )
    grad_back = lax.all_to_all(
        span_section(grad_cols, filt, table_p), "seq", split_axis=1, concat_axis=2, tiled=True
    )
    dw = final_section(grad_back, table_q).reshape(tok, width)
    mixed = (g_part * h4).astype(jnp.bfloat16)
    ds = jnp.concatenate([dw * v_part, gradf * h4, dw * a_part], axis=1).astype(jnp.bfloat16)
    dspad = padded(ds, (("seq", 0),), 1)
    du = (taps[0] * dspad[2:] + taps[1] * dspad[1:-1] + taps[2] * dspad[:-2]).astype(jnp.bfloat16)
    in_grad = jnp.dot(du, w_in.T, preferred_element_type=jnp.float32).astype(jnp.bfloat16)
    dsf = ds.astype(jnp.float32)
    zf = zpad.astype(jnp.float32)
    local_taps = jnp.stack([jnp.sum(dsf * zf[k : k + tok], axis=0) for k in range(3)])
    taps_grad = lax.psum(local_taps, ("dp", "seq")) * factor
    contract = (((0,), (0,)), ((), ()))
    partial_sum = lax.psum_scatter(
        lax.dot_general(rows, du, contract, preferred_element_type=jnp.float32),
        "dp",
        scatter_dimension=0,
        tiled=True,
    )
    w_grad = lax.psum_scatter(partial_sum, "seq", scatter_dimension=1, tiled=True) * factor
    return (mixed[None], in_grad[None], w_grad, taps_grad)


def solution(mesh):
    return jax.shard_map(
        shards,
        mesh=mesh,
        in_specs=(P("dp", "seq", None), P("dp", "seq", None), P(), P(), P(None, "seq", None)),
        out_specs=(P("dp", "seq", None), P("dp", "seq", None), P("dp", "seq"), P()),
        check_vma=False,
    )
```

profile of v0, /device:TPU:2, one launch (start us, length us, event | category | flops | bytes accessed | tf_op | source)
XLA Modules:
  0.0 500.8 jit_solution(6452901341456452620)
XLA Ops:
  8.4 6.4 %convolution_convert_fusion.2 = bf16[512,3072]{1,0:T(8,128)(2,1)S(1)} fusion(bf16[1024,3072]{1,0:T(8,128)(2,1)} %param.7, bf16[1,512,1024]{2,1,0:T(8,128)(2,1)S(1)} %copy-done), kind=kOutput, calls=%fused_computation.22 | convolution fusion | flops 3222798336 | bytes 10485760 | tf_op jit(solution)/shard_map/dot_general | solution.py:72
  14.9 2.0 collective-permute-start
  18.2 3.4 collective-permute-done.1
  21.6 2.5 multiply_add_fusion
  24.2 2.7 copy-done.2
  27.2 1.4 fusion.19
  28.6 2.1 copy.34
  30.7 11.8 %all-to-all-start.2 = ((bf16[1,2,256,1024]{3,1,0,2:T(2,128)(2,1)}), bf16[1,2,256,1024]{3,1,0,2:T(2,128)(2,1)S(1)}, u32[]{:S(2)}, u32[]{:S(2)}) async-start(bf16[1,2,256,1024]{3,1,0,2:T(2,128)(2,1)} %copy.34), calls=%async_computation.2 | async-start | bytes 2097152 | tf_op jit(solution)/shard_map/all_to_all | solution.py:92
  42.6 1.6 reshape.130
  44.2 26.7 %all-to-all-done.2 = bf16[1,2,256,1024]{3,1,0,2:T(2,128)(2,1)S(1)} async-done(((bf16[1,2,256,1024]{3,1,0,2:T(2,128)(2,1)}), bf16[1,2,256,1024]{3,1,0,2:T(2,128)(2,1)S(1)}, u32[]{:S(2)}, u32[]{:S(2)}) %all-to-all-start.2) | async-done | bytes 1048608 | tf_op jit(solution)/shard_map/all_to_all | solution.py:92
  71.2 1.6 copy.47
  72.8 3.8 convolution_convert_fusion
  76.7 2.0 copy.48
  78.7 32.2 %all_to_all.60 = bf16[1,64,8,1024]{3,2,0,1:T(8,128)(2,1)S(1)} all-to-all(bf16[1,64,8,1024]{3,2,0,1:T(8,128)(2,1)S(1)} %bitcast_bitcast_fusion), channel_id=1, replica_groups=mesh['dp'=8,'seq'=32] {'seq'}, dimensions={1} | all-to-all | bytes 2097152 | tf_op jit(solution)/shard_map/all_to_all | solution.py:99
  112.3 2.2 fusion.14
  114.5 2.4 fusion.18
  116.9 3.7 copy.27
  120.6 32.4 %all_to_all.61 = bf16[1,2,256,1024]{3,1,0,2:T(2,128)(2,1)S(1)} all-to-all(bf16[1,2,256,1024]{3,1,0,2:T(2,128)(2,1)} %copy.27), channel_id=1, replica_groups=mesh['dp'=8,'seq'=32] {'seq'}, dimensions={2} | all-to-all | bytes 2097152 | tf_op jit(solution)/shard_map/all_to_all | solution.py:81
  153.4 1.6 copy.45
  155.0 3.2 convolution_convert_fusion.1
  158.2 1.9 copy.46
  160.2 32.4 %all_to_all.62 = bf16[1,64,8,1024]{3,2,0,1:T(8,128)(2,1)S(1)} all-to-all(bf16[1,64,8,1024]{3,2,0,1:T(8,128)(2,1)S(1)} %bitcast_bitcast_fusion.1), channel_id=1, replica_groups=mesh['dp'=8,'seq'=32] {'seq'}, dimensions={1} | all-to-all | bytes 2097152 | tf_op jit(solution)/shard_map/all_to_all | solution.py:88
  193.9 3.2 fusion.13
  198.7 3.0 collective-permute-start.3
  202.6 12.4 %convolution_bitcast_fusion.2 = f32[1024,3072]{0,1:T(8,128)} fusion(bf16[1,512,1024]{2,1,0:T(8,128)(2,1)S(1)} %copy-done, bf16[1,3072]{1,0:T(2,128)(2,1)S(1)} %collective-permute-done.3, bf16[512,1024]{1,0:T(8,128)(2,1)S(1)} %copy-done.6, bf16[512,1024]{1,0:T(8,128)(2,1)S(1)} %get-tuple-element.14, bf16[512,1024]{1,0:T(8,128)(2,1)S(1)} %copy-done.5, ...), kind=kOutput, calls=%fused_computation.14 | convolution fusion | flops 3265265664 | bytes 16826368 | tf_op jit(solution)/shard_map/dot_general | solution.py:114
  215.3 5.5 %maximum_convert_fusion = f32[514,3072]{1,0:T(8,128)} fusion(bf16[1,3072]{1,0:T(2,128)(2,1)S(1)} %collective-permute-done.1, bf16[512,3072]{1,0:T(8,128)(2,1)} %copy-done.4, bf16[1,3072]{1,0:T(2,128)(2,1)S(1)} %collective-permute-done), kind=kLoop, calls=%fused_computation.23 | loop fusion | flops 9474048 | bytes 9474048 | tf_op jit(solution)/shard_map/convert_element_type | solution.py:109
  220.7 152.5 %reduce-scatter.3.cloned.1.call-done = f32[128,3072]{0,1:T(8,128)} async-done(((f32[1024,3072]{0,1:T(8,128)}), f32[128,3072]{0,1:T(8,128)}) %reduce-scatter.3.cloned.1.call-update) | async-done | bytes 1572880 | tf_op jit(solution)/shard_map/reduce_scatter | solution.py:113
  373.3 9.3 %fusion.9 = (f32[3072]{0:T(1024)S(1)}, f32[3072]{0:T(1024)S(1)}, f32[3072]{0:T(1024)S(1)}) fusion(f32[514,3072]{1,0:T(8,128)} %maximum_convert_fusion, bf16[512,1024]{1,0:T(8,128)(2,1)S(1)} %copy-done.6, bf16[512,1024]{1,0:T(8,128)(2,1)S(1)} %copy-done.8, bf16[512,1024]{1,0:T(8,128)(2,1)S(1)} %copy-done.5), kind=kLoop, calls=%fused_computation.18 | loop fusion | flops 18865152 | bytes 22056960 | tf_op jit(solution)/shard_map/reduce_sum | solution.py:110
  382.7 75.7 %psum.7 = f32[3,3072]{1,0:T(4,128)S(1)} all-reduce(f32[3,3072]{1,0:T(4,128)S(1)} %pad_maximum_fusion.9), channel_id=1, replica_groups=mesh['dp'=8,'seq'=32] {'dp','seq'}, use_global_device_ids=true, to_apply=%region_5.6 | all-reduce | flops 9216 | bytes 73728 | tf_op jit(solution)/shard_map/psum | solution.py:111
  459.0 11.0 %fusion.17 = bf16[1,512,1024]{2,1,0:T(8,128)(2,1)} fusion(bf16[1024,3072]{1,0:T(8,128)(2,1)} %param.7, bf16[1,3072]{1,0:T(2,128)(2,1)S(1)} %collective-permute-done.3, bf16[512,1024]{1,0:T(8,128)(2,1)S(1)} %copy-done.6, bf16[512,1024]{1,0:T(8,128)(2,1)} %copy-done.7, bf16[512,1024]{1,0:T(8,128)(2,1)S(1)} %copy-done.5, ...), kind=kOutput, calls=%fused_computation.47 | convolution fusion | flops 3265789952 | bytes 10534912 | tf_op jit(solution)/shard_map/dot_general | solution.py:107
  470.0 22.5 %reduce-scatter.5.cloned.1.call-done = f32[128,96]{0,1:T(8,128)} async-done(((f32[128,3072]{0,1:T(8,128)}), f32[128,96]{0,1:T(8,128)}) %reduce-scatter.5.cloned.1.call-update) | async-done | bytes 49168 | tf_op jit(solution)/shard_map/reduce_scatter | solution.py:119
  492.5 1.4 broadcast_multiply_fusion.1
  (56 shorter events, 9.9 us)
Async XLA Ops:
  7.2 1.2 copy-start
  7.2 11.0 %copy-start.12 = (f32[3,3072]{1,0:T(4,128)S(1)}, f32[3,3072]{1,0:T(4,128)}, u32[]{:S(2)}) copy-start(f32[3,3072]{1,0:T(4,128)} %param.8) | copy-start | bytes 110596
  14.8 12.4 %copy-start.4 = (bf16[512,3072]{1,0:T(8,128)(2,1)}, bf16[512,3072]{1,0:T(8,128)(2,1)S(1)}, u32[]{:S(2)}) copy-start(bf16[512,3072]{1,0:T(8,128)(2,1)S(1)} %convolution_convert_fusion.2) | copy-start | bytes 9437188
  14.8 12.0 %copy-start.9 = (bf16[1,512,1024]{2,1,0:T(8,128)(2,1)S(1)}, bf16[1,512,1024]{2,1,0:T(8,128)(2,1)}, u32[]{:S(2)}) copy-start(bf16[1,512,1024]{2,1,0:T(8,128)(2,1)} %param.6) | copy-start | bytes 3145732
  14.9 3.4 collective-permute-start
  16.9 4.8 collective-permute-start.1
  24.2 2.7 copy-start.2
  26.8 15.7 %copy-start.11 = (bf16[64,8,1024]{2,1,0:T(8,128)(2,1)S(1)}, bf16[64,8,1024]{2,1,0:T(8,128)(2,1)}, u32[]{:S(2)}) copy-start(bf16[64,8,1024]{2,1,0:T(8,128)(2,1)} %param.9) | copy-start | bytes 3145732
  30.7 40.1 %all-to-all-start.2 = ((bf16[1,2,256,1024]{3,1,0,2:T(2,128)(2,1)}), bf16[1,2,256,1024]{3,1,0,2:T(2,128)(2,1)S(1)}, u32[]{:S(2)}, u32[]{:S(2)}) async-start(bf16[1,2,256,1024]{3,1,0,2:T(2,128)(2,1)} %copy.34), calls=%async_computation.2 | async-start | bytes 2097152 | tf_op jit(solution)/shard_map/all_to_all | solution.py:92
  42.5 330.8 %reduce-scatter.3.cloned.1.call-start = ((), (), s32[]{:S(2)}) async-start(), calls=%async_computation.6 | async-start | bytes 14155776 | tf_op jit(solution)/shard_map/reduce_scatter | solution.py:113
  71.2 41.1 %slice-start = ((s8[6291456]{0:T(1024)(128)(4,1)}), s8[2097152]{0:T(1024)(128)(4,1)S(1)}, s32[]{:S(2)}) async-start(s8[6291456]{0:T(1024)(128)(4,1)} %bitcast.146), calls=%async_computation.8 | async-start | bytes 4194304
  76.7 35.6 %slice-start.1 = ((s8[6291456]{0:T(1024)(128)(4,1)}), s8[4194304]{0:T(1024)(128)(4,1)S(1)}, s32[]{:S(2)}) async-start(s8[6291456]{0:T(1024)(128)(4,1)} %bitcast.146), calls=%async_computation.9 | async-start | bytes 8388608
  114.5 40.5 %copy-start.3 = (f32[1,64,8192]{2,1,0:T(8,128)S(1)}, f32[1,64,8192]{2,1,0:T(8,128)}, u32[]{:S(2)}) copy-start(f32[1,64,8192]{2,1,0:T(8,128)} %reshape.130) | copy-start | bytes 6291460
  158.2 35.7 %copy-start.10 = (bf16[1,512,1024]{2,1,0:T(8,128)(2,1)S(1)}, bf16[1,512,1024]{2,1,0:T(8,128)(2,1)}, u32[]{:S(2)}) copy-start(bf16[1,512,1024]{2,1,0:T(8,128)(2,1)} %param.6) | copy-start | bytes 3145732
  160.2 37.0 %copy-start.5 = (bf16[512,1024]{1,0:T(8,128)(2,1)S(1)}, bf16[512,1024]{1,0:T(8,128)(2,1)}, u32[]{:S(2)}) copy-start(bf16[512,1024]{1,0:T(8,128)(2,1)} %get-tuple-element.7) | copy-start | bytes 3145732
  160.2 37.0 %copy-start.6 = (bf16[512,1024]{1,0:T(8,128)(2,1)S(1)}, bf16[512,1024]{1,0:T(8,128)(2,1)}, u32[]{:S(2)}) copy-start(bf16[512,1024]{1,0:T(8,128)(2,1)} %get-tuple-element.8) | copy-start | bytes 3145732
  197.1 5.5 %copy-start.7 = (bf16[512,1024]{1,0:T(8,128)(2,1)}, bf16[512,1024]{1,0:T(8,128)(2,1)S(1)}, u32[]{:S(2)}) copy-start(bf16[512,1024]{1,0:T(8,128)(2,1)S(1)} %get-tuple-element.14) | copy-start | bytes 3145732
  197.4 4.3 collective-permute-start.2
  198.7 3.9 collective-permute-start.3
  215.0 158.3 %copy-start.8 = (bf16[512,1024]{1,0:T(8,128)(2,1)S(1)}, bf16[512,1024]{1,0:T(8,128)(2,1)}, u32[]{:S(2)}) copy-start(bf16[512,1024]{1,0:T(8,128)(2,1)} %copy-done.7) | copy-start | bytes 3145732
  215.0 277.5 %reduce-scatter.5.cloned.1.call-start = ((), (), s32[]{:S(2)}) async-start(), calls=%async_computation.7 | async-start | bytes 1622016 | tf_op jit(solution)/shard_map/reduce_scatter | solution.py:119
  459.0 35.0 %copy-start.1 = (bf16[1,512,1024]{2,1,0:T(8,128)(2,1)S(1)}, bf16[1,512,1024]{2,1,0:T(8,128)(2,1)}, u32[]{:S(2)}) copy-start(bf16[1,512,1024]{2,1,0:T(8,128)(2,1)} %param.5) | copy-start | bytes 3145732
Sparse Core Ops, SparseCore 0:
  215.1 158.0 reduce-scatter.2
  375.9 116.5 reduce-scatter.4
where the time goes:
time: 502 us; the launch traced here: 501 us
  waiting for transfers between devices  206 us (41%)
  blocking collectives  173 us (34%)
  matrix products  43.3 us (9%)
  other arithmetic  25.5 us (5%)
  starting transfers between devices  19.7 us (4%)
  local copies, waits for them, and re-layouts  19.3 us (4%)
  between operations  14.4 us (3%)
    reduce_scatter x1, waiting for transfers between devices, shards(): lax.psum_scatter(lax.dot_general(rows, du, contract, preferred_element_ty...  153 us
    psum x1, blocking collectives, shards(): taps_grad = lax.psum(local_taps, ('dp', 'seq')) * factor  75.7 us
    all_to_all x1, blocking collectives, shards(): lax.all_to_all(block_section(w.reshape(1, nblocks, BLK, width), table_q),...  32.4 us
    all_to_all x1, blocking collectives, shards(): lax.all_to_all(span_section(columns, filt, table_p), 'seq', split_axis=1,...  32.4 us
    all_to_all x1, blocking collectives, shards(): lax.all_to_all(span_section(grad_cols, filt, table_p), 'seq', split_axis=...  32.2 us
    all_to_all x1, waiting for transfers between devices, shards(): lax.all_to_all(block_section(e4.reshape(1, nblocks, BLK, width), table_q)...  26.7 us
    reduce_scatter x1, waiting for transfers between devices, shards(): lax.psum_scatter(partial_sum, 'seq', scatter_dimension=1, tiled=True)  22.5 us
    dot_general x1, matrix products, shards(): lax.dot_general(rows, du, contract, preferred_element_type=jnp.float32)  12.4 us
  transfers between devices with their start and end apart: 7, of which 5 were waited for; matrix products, arithmetic and copies ran while one was open for 6% of the time, Pallas kernels for 0%

commit v1 on v0

--- a/solution.py
+++ b/solution.py
@@ -1,3 +1,4 @@
+import functools
 import math
 import jax
 import jax.numpy as jnp
@@ -5,6 +6,15 @@
 from jax.sharding import PartitionSpec as P
 
 BLK = 256
+
+
+def ticks_map(values, mesh_ax, chip_axis):
+    for q in (mesh_ax, chip_axis):
+        values = jax.lax.psum(values, axis_name=q)
+    return values
+
+
+launch_routes_all = functools.partial(ticks_map, mesh_ax="seq", chip_axis="dp")
 
 
 def padded(cells, sides, width):
@@ -108,7 +118,7 @@
     dsf = ds.astype(jnp.float32)
     zf = zpad.astype(jnp.float32)
     local_taps = jnp.stack([jnp.sum(dsf * zf[k : k + tok], axis=0) for k in range(3)])
-    taps_grad = lax.psum(local_taps, ("dp", "seq")) * factor
+    taps_grad = launch_routes_all(local_taps) * factor
     contract = (((0,), (0,)), ((), ()))
     partial_sum = lax.psum_scatter(
         lax.dot_general(rows, du, contract, preferred_element_type=jnp.float32),

time: 502 us -> 549 us (1.094)
  blocking collectives: 173 us -> 242 us
  waiting for transfers between devices: 206 us -> 184 us
    psum x1 -> x2, blocking collectives: 75.7 us -> 145 us  [ticks_map(): values = jax.lax.psum(values, axis_name=q)]
    reduce_scatter x1, waiting for transfers between devices: 22.5 us -> 0.01 us  [shards(): lax.psum_scatter(partial_sum, 'seq', scatter_dimension=1, tiled=True)]
  transfers between devices with their start and end apart: 7 -> 7, of which waited for: 5 -> 4; matrix products, arithmetic and copies ran while one was open for 6% -> 5% of each run, Pallas kernels for 0% -> 0%
where the time goes in v1:
time: 549 us; the launch traced here: 548 us
  blocking collectives  242 us (44%)
  waiting for transfers between devices  184 us (34%)
  matrix products  43.2 us (8%)
  other arithmetic  25.5 us (5%)
  starting transfers between devices  19.7 us (4%)
  local copies, waits for them, and re-layouts  19.3 us (4%)
  between operations  14.4 us (3%)
    reduce_scatter x1, waiting for transfers between devices, shards(): lax.psum_scatter(lax.dot_general(rows, du, contract, preferred_element_ty...  153 us
    psum x2, blocking collectives, ticks_map(): values = jax.lax.psum(values, axis_name=q)  145 us
    all_to_all x1, blocking collectives, shards(): lax.all_to_all(block_section(w.reshape(1, nblocks, BLK, width), table_q),...  32.5 us
    all_to_all x1, blocking collectives, shards(): lax.all_to_all(span_section(columns, filt, table_p), 'seq', split_axis=1,...  32.4 us
    all_to_all x1, blocking collectives, shards(): lax.all_to_all(span_section(grad_cols, filt, table_p), 'seq', split_axis=...  32.2 us
    all_to_all x1, waiting for transfers between devices, shards(): lax.all_to_all(block_section(e4.reshape(1, nblocks, BLK, width), table_q)...  26.7 us
    dot_general x1, matrix products, shards(): lax.dot_general(rows, du, contract, preferred_element_type=jnp.float32)  12.3 us
    all_to_all x1, starting transfers between devices, shards(): lax.all_to_all(block_section(e4.reshape(1, nblocks, BLK, width), table_q)...  11.8 us
  transfers between devices with their start and end apart: 7, of which 4 were waited for; matrix products, arithmetic and copies ran while one was open for 5% of the time, Pallas kernels for 0%

profile of v1, /device:TPU:2, one launch (start us, length us, event | category | flops | bytes accessed | tf_op | source)
XLA Modules:
  0.0 547.6 jit_solution(397851486052933344)
XLA Ops:
  8.4 6.4 %convolution_convert_fusion.2 = bf16[512,3072]{1,0:T(8,128)(2,1)S(1)} fusion(bf16[1024,3072]{1,0:T(8,128)(2,1)} %param.7, bf16[1,512,1024]{2,1,0:T(8,128)(2,1)S(1)} %copy-done), kind=kOutput, calls=%fused_computation.22 | convolution fusion | flops 3222798336 | bytes 10485760 | tf_op jit(solution)/shard_map/dot_general | solution.py:82
  14.9 2.0 collective-permute-start
  18.2 3.4 collective-permute-done.1
  21.6 2.5 multiply_add_fusion
  24.2 2.7 copy-done.2
  27.2 1.4 fusion.19
  28.6 2.1 copy.34
  30.7 11.8 %all-to-all-start.2 = ((bf16[1,2,256,1024]{3,1,0,2:T(2,128)(2,1)}), bf16[1,2,256,1024]{3,1,0,2:T(2,128)(2,1)S(1)}, u32[]{:S(2)}, u32[]{:S(2)}) async-start(bf16[1,2,256,1024]{3,1,0,2:T(2,128)(2,1)} %copy.34), calls=%async_computation.2 | async-start | bytes 2097152 | tf_op jit(solution)/shard_map/all_to_all | solution.py:102
  42.6 1.6 reshape.130
  44.1 26.7 %all-to-all-done.2 = bf16[1,2,256,1024]{3,1,0,2:T(2,128)(2,1)S(1)} async-done(((bf16[1,2,256,1024]{3,1,0,2:T(2,128)(2,1)}), bf16[1,2,256,1024]{3,1,0,2:T(2,128)(2,1)S(1)}, u32[]{:S(2)}, u32[]{:S(2)}) %all-to-all-start.2) | async-done | bytes 1048608 | tf_op jit(solution)/shard_map/all_to_all | solution.py:102
  71.2 1.6 copy.47
  72.8 3.8 convolution_convert_fusion
  76.7 2.0 copy.48
  78.7 32.2 %all_to_all.60 = bf16[1,64,8,1024]{3,2,0,1:T(8,128)(2,1)S(1)} all-to-all(bf16[1,64,8,1024]{3,2,0,1:T(8,128)(2,1)S(1)} %bitcast_bitcast_fusion), channel_id=1, replica_groups=mesh['dp'=8,'seq'=32] {'seq'}, dimensions={1} | all-to-all | bytes 2097152 | tf_op jit(solution)/shard_map/all_to_all | solution.py:109
  112.3 2.2 fusion.14
  114.6 2.4 fusion.18
  116.9 3.7 copy.27
  120.7 32.5 %all_to_all.61 = bf16[1,2,256,1024]{3,1,0,2:T(2,128)(2,1)S(1)} all-to-all(bf16[1,2,256,1024]{3,1,0,2:T(2,128)(2,1)} %copy.27), channel_id=1, replica_groups=mesh['dp'=8,'seq'=32] {'seq'}, dimensions={2} | all-to-all | bytes 2097152 | tf_op jit(solution)/shard_map/all_to_all | solution.py:91
  153.5 1.6 copy.45
  155.1 3.2 convolution_convert_fusion.1
  158.2 1.9 copy.46
  160.3 32.4 %all_to_all.62 = bf16[1,64,8,1024]{3,2,0,1:T(8,128)(2,1)S(1)} all-to-all(bf16[1,64,8,1024]{3,2,0,1:T(8,128)(2,1)S(1)} %bitcast_bitcast_fusion.1), channel_id=1, replica_groups=mesh['dp'=8,'seq'=32] {'seq'}, dimensions={1} | all-to-all | bytes 2097152 | tf_op jit(solution)/shard_map/all_to_all | solution.py:98
  194.0 3.2 fusion.13
  198.8 3.0 collective-permute-start.3
  202.7 12.3 %convolution_bitcast_fusion.2 = f32[1024,3072]{0,1:T(8,128)} fusion(bf16[1,512,1024]{2,1,0:T(8,128)(2,1)S(1)} %copy-done, bf16[1,3072]{1,0:T(2,128)(2,1)S(1)} %collective-permute-done.3, bf16[512,1024]{1,0:T(8,128)(2,1)S(1)} %copy-done.6, bf16[512,1024]{1,0:T(8,128)(2,1)S(1)} %get-tuple-element.14, bf16[512,1024]{1,0:T(8,128)(2,1)S(1)} %copy-done.5, ...), kind=kOutput, calls=%fused_computation.14 | convolution fusion | flops 3265265664 | bytes 16826368 | tf_op jit(solution)/shard_map/dot_general | solution.py:124
  215.3 5.5 %maximum_convert_fusion = f32[514,3072]{1,0:T(8,128)} fusion(bf16[1,3072]{1,0:T(2,128)(2,1)S(1)} %collective-permute-done.1, bf16[512,3072]{1,0:T(8,128)(2,1)} %copy-done.4, bf16[1,3072]{1,0:T(2,128)(2,1)S(1)} %collective-permute-done), kind=kLoop, calls=%fused_computation.23 | loop fusion | flops 9474048 | bytes 9474048 | tf_op jit(solution)/shard_map/convert_element_type | solution.py:119
  220.8 152.6 %reduce-scatter.3.cloned.1.call-done = f32[128,3072]{0,1:T(8,128)} async-done(((f32[1024,3072]{0,1:T(8,128)}), f32[128,3072]{0,1:T(8,128)}) %reduce-scatter.3.cloned.1.call-update) | async-done | bytes 1572880 | tf_op jit(solution)/shard_map/reduce_scatter | solution.py:123
  373.4 9.3 %fusion.9 = (f32[3072]{0:T(1024)S(1)}, f32[3072]{0:T(1024)S(1)}, f32[3072]{0:T(1024)S(1)}) fusion(f32[514,3072]{1,0:T(8,128)} %maximum_convert_fusion, bf16[512,1024]{1,0:T(8,128)(2,1)S(1)} %copy-done.6, bf16[512,1024]{1,0:T(8,128)(2,1)S(1)} %copy-done.8, bf16[512,1024]{1,0:T(8,128)(2,1)S(1)} %copy-done.5), kind=kLoop, calls=%fused_computation.18 | loop fusion | flops 18865152 | bytes 22056960 | tf_op jit(solution)/shard_map/reduce_sum | solution.py:120
  382.8 106.6 %psum.14 = f32[3,3072]{1,0:T(4,128)S(1)} all-reduce(f32[3,3072]{1,0:T(4,128)S(1)} %pad_maximum_fusion.9), channel_id=1, replica_groups=mesh['dp'=8,'seq'=32] {'seq'}, use_global_device_ids=true, to_apply=%region_5.6 | all-reduce | flops 9216 | bytes 73728 | tf_op jit(solution)/shard_map/psum | solution.py:13
  489.4 38.3 %psum.15 = f32[3,3072]{1,0:T(4,128)S(1)} all-reduce(f32[3,3072]{1,0:T(4,128)S(1)} %psum.14), channel_id=1, replica_groups=mesh['dp'=8,'seq'=32] {'dp'}, use_global_device_ids=true, to_apply=%region_6.7 | all-reduce | flops 9216 | bytes 73728 | tf_op jit(solution)/shard_map/psum | solution.py:13
  528.3 11.0 %fusion.17 = bf16[1,512,1024]{2,1,0:T(8,128)(2,1)} fusion(bf16[1024,3072]{1,0:T(8,128)(2,1)} %param.7, bf16[1,3072]{1,0:T(2,128)(2,1)S(1)} %collective-permute-done.3, bf16[512,1024]{1,0:T(8,128)(2,1)S(1)} %copy-done.6, bf16[512,1024]{1,0:T(8,128)(2,1)} %copy-done.7, bf16[512,1024]{1,0:T(8,128)(2,1)S(1)} %copy-done.5, ...), kind=kOutput, calls=%fused_computation.47 | convolution fusion | flops 3265789952 | bytes 10534912 | tf_op jit(solution)/shard_map/dot_general | solution.py:117
  539.3 1.4 broadcast_multiply_fusion.1
  (57 shorter events, 9.9 us)
Async XLA Ops:
  7.2 1.2 copy-start
  7.2 11.0 %copy-start.12 = (f32[3,3072]{1,0:T(4,128)S(1)}, f32[3,3072]{1,0:T(4,128)}, u32[]{:S(2)}) copy-start(f32[3,3072]{1,0:T(4,128)} %param.8) | copy-start | bytes 110596
  14.8 12.4 %copy-start.4 = (bf16[512,3072]{1,0:T(8,128)(2,1)}, bf16[512,3072]{1,0:T(8,128)(2,1)S(1)}, u32[]{:S(2)}) copy-start(bf16[512,3072]{1,0:T(8,128)(2,1)S(1)} %convolution_convert_fusion.2) | copy-start | bytes 9437188
  14.8 12.0 %copy-start.9 = (bf16[1,512,1024]{2,1,0:T(8,128)(2,1)S(1)}, bf16[1,512,1024]{2,1,0:T(8,128)(2,1)}, u32[]{:S(2)}) copy-start(bf16[1,512,1024]{2,1,0:T(8,128)(2,1)} %param.6) | copy-start | bytes 3145732
  14.9 3.4 collective-permute-start
  16.9 4.8 collective-permute-start.1
  24.2 2.7 copy-start.2
  26.8 15.7 %copy-start.11 = (bf16[64,8,1024]{2,1,0:T(8,128)(2,1)S(1)}, bf16[64,8,1024]{2,1,0:T(8,128)(2,1)}, u32[]{:S(2)}) copy-start(bf16[64,8,1024]{2,1,0:T(8,128)(2,1)} %param.9) | copy-start | bytes 3145732
  30.7 40.2 %all-to-all-start.2 = ((bf16[1,2,256,1024]{3,1,0,2:T(2,128)(2,1)}), bf16[1,2,256,1024]{3,1,0,2:T(2,128)(2,1)S(1)}, u32[]{:S(2)}, u32[]{:S(2)}) async-start(bf16[1,2,256,1024]{3,1,0,2:T(2,128)(2,1)} %copy.34), calls=%async_computation.2 | async-start | bytes 2097152 | tf_op jit(solution)/shard_map/all_to_all | solution.py:102
  42.5 330.9 %reduce-scatter.3.cloned.1.call-start = ((), (), s32[]{:S(2)}) async-start(), calls=%async_computation.6 | async-start | bytes 14155776 | tf_op jit(solution)/shard_map/reduce_scatter | solution.py:123
  71.2 41.1 %slice-start = ((s8[6291456]{0:T(1024)(128)(4,1)}), s8[2097152]{0:T(1024)(128)(4,1)S(1)}, s32[]{:S(2)}) async-start(s8[6291456]{0:T(1024)(128)(4,1)} %bitcast.146), calls=%async_computation.8 | async-start | bytes 4194304
  76.7 35.7 %slice-start.1 = ((s8[6291456]{0:T(1024)(128)(4,1)}), s8[4194304]{0:T(1024)(128)(4,1)S(1)}, s32[]{:S(2)}) async-start(s8[6291456]{0:T(1024)(128)(4,1)} %bitcast.146), calls=%async_computation.9 | async-start | bytes 8388608
  114.6 40.5 %copy-start.3 = (f32[1,64,8192]{2,1,0:T(8,128)S(1)}, f32[1,64,8192]{2,1,0:T(8,128)}, u32[]{:S(2)}) copy-start(f32[1,64,8192]{2,1,0:T(8,128)} %reshape.130) | copy-start | bytes 6291460
  158.2 35.7 %copy-start.10 = (bf16[1,512,1024]{2,1,0:T(8,128)(2,1)S(1)}, bf16[1,512,1024]{2,1,0:T(8,128)(2,1)}, u32[]{:S(2)}) copy-start(bf16[1,512,1024]{2,1,0:T(8,128)(2,1)} %param.6) | copy-start | bytes 3145732
  160.2 37.0 %copy-start.5 = (bf16[512,1024]{1,0:T(8,128)(2,1)S(1)}, bf16[512,1024]{1,0:T(8,128)(2,1)}, u32[]{:S(2)}) copy-start(bf16[512,1024]{1,0:T(8,128)(2,1)} %get-tuple-element.7) | copy-start | bytes 3145732
  160.2 37.0 %copy-start.6 = (bf16[512,1024]{1,0:T(8,128)(2,1)S(1)}, bf16[512,1024]{1,0:T(8,128)(2,1)}, u32[]{:S(2)}) copy-start(bf16[512,1024]{1,0:T(8,128)(2,1)} %get-tuple-element.8) | copy-start | bytes 3145732
  197.2 5.5 copy-start.7
  197.5 4.3 collective-permute-start.2
  198.8 3.9 collective-permute-start.3
  215.0 158.3 %copy-start.8 = (bf16[512,1024]{1,0:T(8,128)(2,1)S(1)}, bf16[512,1024]{1,0:T(8,128)(2,1)}, u32[]{:S(2)}) copy-start(bf16[512,1024]{1,0:T(8,128)(2,1)} %copy-done.7) | copy-start | bytes 3145732
  215.0 324.2 %reduce-scatter.5.cloned.1.call-start = ((), (), s32[]{:S(2)}) async-start(), calls=%async_computation.7 | async-start | bytes 1622016 | tf_op jit(solution)/shard_map/reduce_scatter | solution.py:129
  528.3 12.4 %copy-start.1 = (bf16[1,512,1024]{2,1,0:T(8,128)(2,1)S(1)}, bf16[1,512,1024]{2,1,0:T(8,128)(2,1)}, u32[]{:S(2)}) copy-start(bf16[1,512,1024]{2,1,0:T(8,128)(2,1)} %param.5) | copy-start | bytes 3145732
Sparse Core Ops, SparseCore 0:
  215.2 158.1 reduce-scatter.2
  376.0 116.8 reduce-scatter.4
